TPU v7x, 512 devices: a whole 4x8x8 slice. The times are simulated.
512 devices in a mesh: row: 8 (over z_lo, core), bulk: 64 (over z_hi, x, y).
Axes of the slice: x: 4, y: 8, z: 8 (z_hi: 2, z_lo: 4; z = z_hi * 4 + z_lo), core: 2. Of those that a mesh axis runs over, the one named last changes fastest.
Arguments:
- residual_in: float32 [2048, 65536], P('row', 'bulk'), may hold values from -6 to 6
- amplitudes: float32 [2048, 2048], P('row', 'bulk'), may hold values from -6 to 6
- integral_tiles: float32 [4096, 128, 128], P('bulk', 'row'), may hold values from -0.1875 to 0.1875
- tile_reader: int32 [4096, 1], P('bulk'), may hold values from 0 to 63; in each aligned block of 64 rows (0 to 63, 64 to 127, ...) at most 2 rows name the same one
- tile_k: int32 [4096], P('bulk'), may hold values from 0 to 15
- tile_column: int32 [4096], P('bulk'), may hold values from 0 to 7
Outputs:
- residual_out: float32 [2048, 65536], P('row', 'bulk')
Inputs may be any that keep to these rules, and one draw needn't show every extreme that they name: `tile_reader`: among the 64 tiles stored on one index of bulk (aligned blocks of 64 entries), at most 2 name the same reader; some block has exactly 2 for some reader.
All inputs are finite; a program needn't handle non-finite values.
Results may differ from a plain program's by a relative error of at most 0.0003.
Values sent between devices are 32-bit elements; how exact they have to be, the bound alone decides.
A program may use at most 64 MiB of HBM per device.

v0:
```python
import jax
import jax.numpy as jnp
from jax import lax
from jax.sharding import PartitionSpec as P

KT = 16
CT = 8
SLOT = 2


def bucket_slots(tile_reader, tile_k, tile_column, targets, slots):
    readers = tile_reader[:, 0]
    matches = (readers[:, None] == jnp.arange(targets, dtype=jnp.int32)[None, :]).astype(jnp.int32)
    ordinal = jnp.cumsum(matches, axis=0) - matches
    position = jnp.sum(ordinal * matches, axis=1)
    select = matches.T[:, None, :] * (
        position[None, None, :] == jnp.arange(slots, dtype=jnp.int32)[None, :, None]
    ).astype(jnp.int32)
    filled = jnp.sum(select, axis=2)
    slot_tile = jnp.sum(select * tile_k[None, None, :], axis=2) + filled - 1
    slot_column = jnp.sum(select * tile_column[None, None, :], axis=2) + filled - 1
    return (select.astype(jnp.float32), slot_tile, slot_column)


def pair_table(slot_tile, slot_column, tiles_count, column_count):
    tile_hot = (slot_tile[:, None] == jnp.arange(tiles_count, dtype=jnp.int32)[None, :]).astype(
        jnp.float32
    )
    column_hot = (
        slot_column[:, None] == jnp.arange(column_count, dtype=jnp.int32)[None, :]
    ).astype(jnp.float32)
    return (tile_hot[:, :, None] * column_hot[:, None, :]).reshape(
        slot_tile.shape[0], tiles_count * column_count
    )


def place_rows(table, portion, tiles_count, column_count):
    width = portion.shape[2]
    height = portion.shape[1]
    placed = jnp.dot(
        table.T, portion.reshape(portion.shape[0], height * width), precision=lax.Precision.HIGHEST
    )
    placed = placed.reshape(tiles_count, column_count, height, width).transpose(0, 2, 1, 3)
    return placed


def local(residual_in, amplitudes, integral_tiles, tile_reader, tile_k, tile_column):
    targets = lax.axis_size("bulk")
    select, slot_tile, slot_column = bucket_slots(tile_reader, tile_k, tile_column, targets, SLOT)
    width = integral_tiles.shape[2]
    whole_tiles = lax.all_gather(integral_tiles, "row", axis=1, tiled=True)
    outgoing = jnp.einsum("dsj,jpq->dspq", select, whole_tiles, precision=lax.Precision.HIGHEST)
    arrived, arrived_tile, arrived_column = (
        lax.all_to_all(outgoing, "bulk", split_axis=0, concat_axis=0, tiled=True),
        lax.all_to_all(slot_tile, "bulk", split_axis=0, concat_axis=0, tiled=True),
        lax.all_to_all(slot_column, "bulk", split_axis=0, concat_axis=0, tiled=True),
    )
    arrived = arrived.reshape(targets * SLOT, width, width)
    table = pair_table(arrived_tile.reshape(-1), arrived_column.reshape(-1), KT, CT)
    assembled = place_rows(table, arrived, KT, CT)
    dense_block = assembled.reshape(KT * width, CT * width)
    return residual_in + jnp.dot(
        lax.all_gather(amplitudes, "bulk", axis=1, tiled=True),
        dense_block,
        precision=lax.Precision.HIGHEST,
    )


def solution(mesh):
    placed = (
        P("row", "bulk"),
        P("row", "bulk"),
        P("bulk", "row", None),
        P("bulk", None),
        P("bulk"),
        P("bulk"),
    )
    return jax.shard_map(
        local, mesh=mesh, in_specs=placed, out_specs=P("row", "bulk"), check_vma=False
    )
```

profile of v0, /device:TPU:2, one launch (start us, length us, event | category | flops | bytes accessed | tf_op | source)
XLA Modules:
  0.0 432.5 jit_solution(5636964937242267138)
XLA Ops:
  7.4 0.0 all-gather.3.cloned.1.call-start
  7.4 2.0 copy.21
  9.4 0.0 all-gather.3.cloned.1.call-update
  9.4 0.8 fusion.23
  10.2 0.1 reduce_window_sum.11
  10.3 0.8 select_reduce_fusion
  11.2 0.9 fusion.11
  12.0 0.7 copy.19
  12.7 19.1 %all-to-all-start = ((s32[64,1,2]{2,1,0:T(1,128)}), s32[64,1,2]{2,1,0:T(1,128)S(1)}, u32[]{:S(2)}, u32[]{:S(2)}) async-start(s32[64,1,2]{2,1,0:T(1,128)} %copy.19), calls=%async_computation | async-start | bytes 65536 | tf_op jit(solution)/shard_map/all_to_all | solution.py:55
  31.8 0.7 copy.20
  32.5 12.7 %all-to-all-done = s32[64,1,2]{2,1,0:T(1,128)S(1)} async-done(((s32[64,1,2]{2,1,0:T(1,128)}), s32[64,1,2]{2,1,0:T(1,128)S(1)}, u32[]{:S(2)}, u32[]{:S(2)}) %all-to-all-start) | async-done | bytes 544 | tf_op jit(solution)/shard_map/all_to_all | solution.py:55
  45.3 5.4 %all-to-all-start.1 = ((s32[64,1,2]{2,1,0:T(1,128)}), s32[64,1,2]{2,1,0:T(1,128)S(1)}, u32[]{:S(2)}, u32[]{:S(2)}) async-start(s32[64,1,2]{2,1,0:T(1,128)} %copy.20), calls=%async_computation.1 | async-start | bytes 65536 | tf_op jit(solution)/shard_map/all_to_all | solution.py:56
  50.7 23.5 %all-gather.3.cloned.1.call-done = f32[64,128,128]{2,0,1:T(8,128)} async-done(((f32[64,16,128]{2,0,1:T(8,128)}), f32[64,128,128]{2,0,1:T(8,128)}) %all-gather.3.cloned.1.call-update) | async-done | bytes 4194320 | tf_op jit(solution)/shard_map/all_gather | solution.py:51
  74.2 8.7 %fusion.3 = f32[64,2,128,128]{3,0,2,1:T(8,128)S(1)} fusion(f32[64,128,128]{2,0,1:T(8,128)} %all-gather.3.cloned.1.call-done, s32[2,64]{1,0:T(2,128)S(1)} %compare_convert_fusion, s32[64,64]{1,0:T(8,128)S(1)} %get-tuple-element.10), kind=kOutput, calls=%fused_computation.4 | convolution fusion | flops 1610629120 | bytes 12599808 | tf_op jit(solution)/shard_map/dsj,jpq->dspq/dot_general | solution.py:52
  82.9 8.1 %copy.22 = f32[64,2,128,128]{3,2,1,0:T(8,128)} copy(f32[64,2,128,128]{3,0,2,1:T(8,128)S(1)} %fusion.3) | data formatting | bytes 16777216 | tf_op jit(solution)/shard_map/dsj,jpq->dspq/dot_general | solution.py:52
  91.0 0.0 copy-start
  91.0 0.0 all-to-all-done.1
  91.0 13.4 %all-to-all-start.2 = ((f32[64,2,128,128]{3,2,1,0:T(8,128)}), f32[64,2,128,128]{3,2,1,0:T(8,128)}, u32[]{:S(2)}, u32[]{:S(2)}) async-start(f32[64,2,128,128]{3,2,1,0:T(8,128)} %copy.22), calls=%async_computation.2 | async-start | bytes 16777216 | tf_op jit(solution)/shard_map/all_to_all | solution.py:54
  104.4 0.0 all-gather.5.cloned.1.call-start
  104.5 0.5 all-gather.5.cloned.1.call-update
  105.0 0.0 copy-done
  105.0 0.3 copy.24
  105.3 0.5 broadcast.89
  105.9 0.7 reduce.7
  106.6 0.1 eq.92
  106.7 0.7 reduce.6
  107.5 0.1 eq.96
  107.6 236.8 %all-to-all-done.2 = f32[64,2,128,128]{3,2,1,0:T(8,128)} async-done(((f32[64,2,128,128]{3,2,1,0:T(8,128)}), f32[64,2,128,128]{3,2,1,0:T(8,128)}, u32[]{:S(2)}, u32[]{:S(2)}) %all-to-all-start.2) | async-done | bytes 8388640 | tf_op jit(solution)/shard_map/all_to_all | solution.py:54
  344.4 13.2 %copy.39 = f32[16,8,128,128]{3,1,2,0:T(8,128)} copy(f32[16,8,128,128]{3,2,1,0:T(8,128)} %bitcast.23) | data formatting | bytes 16777216
  357.6 9.0 %copy.23 = f32[16384,128]{1,0:T(8,128)} copy(f32[16384,128]{0,1:T(8,128)} %bitcast.53) | data formatting | bytes 16777216 | tf_op jit(solution)/shard_map/dot_general | solution.py:40
  366.6 12.1 %fusion.15 = f32[16,8,128,128]{3,1,2,0:T(8,128)} fusion(f32[128,128,128,1]{2,1,0,3:T(8,128)} %bitcast.52, f32[128,8]{0,1:T(8,128)S(1)} %fusion.25, f32[128,16]{0,1:T(8,128)S(1)} %fusion.24), kind=kOutput, calls=%fused_computation.15 | convolution fusion | flops 3221241856 | bytes 16789504 | tf_op jit(solution)/shard_map/dot_general | solution.py:40
  378.6 28.0 %all-gather.5.cloned.1.call-done = f32[256,2048]{0,1:T(8,128)} async-done(((f32[256,32]{0,1:T(8,128)}), f32[256,2048]{0,1:T(8,128)}) %all-gather.5.cloned.1.call-update) | async-done | bytes 2097168 | tf_op jit(solution)/shard_map/all_gather | solution.py:63
  406.7 17.1 %fusion.8 = f32[256,1024]{0,1:T(8,128)S(1)} fusion(f32[256,1024]{0,1:T(8,128)S(1)} %copy.24, f32[256,2048]{0,1:T(8,128)} %all-gather.5.cloned.1.call-done, f32[256,8,8,128]{3,2,1,0:T(8,128)} %bitcast.51), kind=kOutput, calls=%fused_computation.7 | convolution fusion | flops 6442713088 | bytes 12582912 | tf_op jit(solution)/shard_map/dot_general | solution.py:62
  423.7 1.3 copy.25
  (4 shorter events, 0.0 us)
Async XLA Ops:
  7.4 66.8 %all-gather.3.cloned.1.call-start = ((), (), s32[]{:S(2)}) async-start(), calls=%async_computation.3 | async-start | bytes 4718592 | tf_op jit(solution)/shard_map/all_gather | solution.py:51
  12.7 32.5 %all-to-all-start = ((s32[64,1,2]{2,1,0:T(1,128)}), s32[64,1,2]{2,1,0:T(1,128)S(1)}, u32[]{:S(2)}, u32[]{:S(2)}) async-start(s32[64,1,2]{2,1,0:T(1,128)} %copy.19), calls=%async_computation | async-start | bytes 65536 | tf_op jit(solution)/shard_map/all_to_all | solution.py:55
  45.3 45.7 %all-to-all-start.1 = ((s32[64,1,2]{2,1,0:T(1,128)}), s32[64,1,2]{2,1,0:T(1,128)S(1)}, u32[]{:S(2)}, u32[]{:S(2)}) async-start(s32[64,1,2]{2,1,0:T(1,128)} %copy.20), calls=%async_computation.1 | async-start | bytes 65536 | tf_op jit(solution)/shard_map/all_to_all | solution.py:56
  91.0 14.0 %copy-start = (f32[256,1024]{1,0:T(8,128)S(1)}, f32[256,1024]{1,0:T(8,128)}, u32[]{:S(2)}) copy-start(f32[256,1024]{1,0:T(8,128)} %param.6) | copy-start | bytes 3145732
  91.0 253.4 %all-to-all-start.2 = ((f32[64,2,128,128]{3,2,1,0:T(8,128)}), f32[64,2,128,128]{3,2,1,0:T(8,128)}, u32[]{:S(2)}, u32[]{:S(2)}) async-start(f32[64,2,128,128]{3,2,1,0:T(8,128)} %copy.22), calls=%async_computation.2 | async-start | bytes 16777216 | tf_op jit(solution)/shard_map/all_to_all | solution.py:54
  104.4 302.2 %all-gather.5.cloned.1.call-start = ((), (), s32[]{:S(2)}) async-start(), calls=%async_computation.4 | async-start | bytes 2129920 | tf_op jit(solution)/shard_map/all_gather | solution.py:63
Sparse Core Ops, SparseCore 0:
  10.3 63.8 all-gather.2
Sparse Core Ops, SparseCore 1:
  109.4 297.2 all-gather.4
where the time goes:
time: 433 us; the launch traced here: 432 us
  waiting for transfers between devices  302 us (70%)
  starting transfers between devices  38 us (9%)
  matrix products  37.9 us (9%)
  local copies, waits for them, and re-layouts  36.1 us (8%)
  between operations  15 us (3%)
    all_to_all x1, waiting for transfers between devices, local(): lax.all_to_all(outgoing, 'bulk', split_axis=0, concat_axis=0, tiled=True)  237 us
    all_gather x1, waiting for transfers between devices, local(): lax.all_gather(amplitudes, 'bulk', axis=1, tiled=True)  28 us
    all_gather x1, waiting for transfers between devices, local(): whole_tiles = lax.all_gather(integral_tiles, 'row', axis=1, tiled=True)  23.5 us
    all_to_all x1, starting transfers between devices, local(): lax.all_to_all(slot_tile, 'bulk', split_axis=0, concat_axis=0, tiled=True)  19.1 us
    dot_general x1, matrix products, local(): jnp.dot(lax.all_gather(amplitudes, 'bulk', axis=1, tiled=True), dense_blo...  17.1 us
    unnamed x5, local copies, waits for them, and re-layouts  15.5 us
    all_to_all x1, starting transfers between devices, local(): lax.all_to_all(outgoing, 'bulk', split_axis=0, concat_axis=0, tiled=True)  13.4 us
    all_to_all x1, waiting for transfers between devices, local(): lax.all_to_all(slot_tile, 'bulk', split_axis=0, concat_axis=0, tiled=True)  12.7 us
  transfers between devices with their start and end apart: 5, of which 4 were waited for; matrix products, arithmetic and copies ran while one was open for 13% of the time, Pallas kernels for 0%

commit v1 on v0

--- a/solution.py
+++ b/solution.py
@@ -60,7 +60,9 @@
     assembled = place_rows(table, arrived, KT, CT)
     dense_block = assembled.reshape(KT * width, CT * width)
     return residual_in + jnp.dot(
-        lax.all_gather(amplitudes, "bulk", axis=1, tiled=True),
+        jnp.concatenate(
+            lax.all_to_all(jnp.stack([amplitudes] * lax.axis_size("bulk")), "bulk", 0, 0), axis=1
+        ),
         dense_block,
         precision=lax.Precision.HIGHEST,
     )

time: 433 us -> 396 us (0.915)
  the two profiles are of different devices: /device:TPU:2 before, /device:TPU:142 now
where the time goes in v1:
time: 396 us
  blocking collectives  205 us (52%)
  waiting for transfers between devices  47.6 us (12%)
  starting transfers between devices  46.5 us (12%)
  local copies, waits for them, and re-layouts  40.1 us (10%)
  matrix products  38.6 us (10%)
  between operations  13.5 us (3%)
  other arithmetic  4.07 us (1%)
    all_to_all x1, blocking collectives, local(): lax.all_to_all(outgoing, 'bulk', split_axis=0, concat_axis=0, tiled=True)  205 us
    all_to_all x1, starting transfers between devices, local(): lax.all_to_all(jnp.stack([amplitudes] * lax.axis_size('bulk')), 'bulk', 0...  22.4 us
    all_gather x1, waiting for transfers between devices, local(): whole_tiles = lax.all_gather(integral_tiles, 'row', axis=1, tiled=True)  19.8 us
    dot_general x1, matrix products, local(): jnp.dot(jnp.concatenate(lax.all_to_all(jnp.stack([amplitudes] * lax.axis_...  17.8 us
    all_to_all x1, starting transfers between devices, local(): lax.all_to_all(slot_tile, 'bulk', split_axis=0, concat_axis=0, tiled=True)  17.2 us
    unnamed x5, local copies, waits for them, and re-layouts  16.7 us
    all_to_all x1, waiting for transfers between devices, local(): lax.all_to_all(jnp.stack([amplitudes] * lax.axis_size('bulk')), 'bulk', 0...  16.5 us
    dot_general x1, matrix products, place_rows(): jnp.dot(table.T, portion.reshape(portion.shape[0], height * width), preci...  12.1 us
  transfers between devices with their start and end apart: 4, of which 3 were waited for; matrix products, arithmetic and copies ran while one was open for 15% of the time, Pallas kernels for 0%

profile of v1, /device:TPU:142, one launch (start us, length us, event | category | flops | bytes accessed | tf_op | source)
XLA Modules:
  0.0 395.6 jit_solution(8894293371314375349)
XLA Ops:
  6.5 0.0 all-gather.2.cloned.1.call-start
  6.5 2.0 copy.22
  8.5 0.0 all-gather.2.cloned.1.call-update
  8.6 0.8 fusion.23
  9.4 0.1 reduce_window_sum.11
  9.5 0.8 select_reduce_fusion
  10.3 0.9 fusion.11
  11.2 0.7 copy.20
  11.9 17.2 %all-to-all-start = ((s32[64,1,2]{2,1,0:T(1,128)}), s32[64,1,2]{2,1,0:T(1,128)S(1)}, u32[]{:S(2)}, u32[]{:S(2)}) async-start(s32[64,1,2]{2,1,0:T(1,128)} %copy.20), calls=%async_computation | async-start | bytes 65536 | tf_op jit(solution)/shard_map/all_to_all | solution.py:55
  29.1 0.7 copy.21
  29.8 11.3 %all-to-all-done = s32[64,1,2]{2,1,0:T(1,128)S(1)} async-done(((s32[64,1,2]{2,1,0:T(1,128)}), s32[64,1,2]{2,1,0:T(1,128)S(1)}, u32[]{:S(2)}, u32[]{:S(2)}) %all-to-all-start) | async-done | bytes 544 | tf_op jit(solution)/shard_map/all_to_all | solution.py:55
  41.1 6.9 %all-to-all-start.1 = ((s32[64,1,2]{2,1,0:T(1,128)}), s32[64,1,2]{2,1,0:T(1,128)S(1)}, u32[]{:S(2)}, u32[]{:S(2)}) async-start(s32[64,1,2]{2,1,0:T(1,128)} %copy.21), calls=%async_computation.1 | async-start | bytes 65536 | tf_op jit(solution)/shard_map/all_to_all | solution.py:56
  48.0 19.8 %all-gather.2.cloned.1.call-done = f32[64,128,128]{2,0,1:T(8,128)} async-done(((f32[64,16,128]{2,0,1:T(8,128)}), f32[64,128,128]{2,0,1:T(8,128)}) %all-gather.2.cloned.1.call-update) | async-done | bytes 4194320 | tf_op jit(solution)/shard_map/all_gather | solution.py:51
  67.8 8.7 %fusion.3 = f32[64,2,128,128]{3,0,2,1:T(8,128)S(1)} fusion(f32[64,128,128]{2,0,1:T(8,128)} %all-gather.2.cloned.1.call-done, s32[2,64]{1,0:T(2,128)S(1)} %compare_convert_fusion, s32[64,64]{1,0:T(8,128)S(1)} %get-tuple-element.10), kind=kOutput, calls=%fused_computation.4 | convolution fusion | flops 1610629120 | bytes 12599808 | tf_op jit(solution)/shard_map/dsj,jpq->dspq/dot_general | solution.py:52
  76.6 8.1 %copy.23 = f32[64,2,128,128]{3,2,1,0:T(8,128)} copy(f32[64,2,128,128]{3,0,2,1:T(8,128)S(1)} %fusion.3) | data formatting | bytes 16777216 | tf_op jit(solution)/shard_map/dsj,jpq->dspq/dot_general | solution.py:52
  84.7 0.0 copy-start
  84.7 0.0 all-to-all-done.1
  84.7 205.2 %all_to_all.22 = f32[64,2,128,128]{3,2,1,0:T(8,128)} all-to-all(f32[64,2,128,128]{3,2,1,0:T(8,128)} %copy.23), channel_id=1, replica_groups=mesh['row'=8,'bulk'=64] {'bulk'}, dimensions={0} | all-to-all | bytes 16777216 | tf_op jit(solution)/shard_map/all_to_all | solution.py:54
  289.8 0.0 copy-done
  289.8 1.6 stack.2
  291.5 22.4 %all-to-all-start.3 = ((f32[64,256,32]{1,2,0:T(8,128)}), f32[64,256,32]{1,2,0:T(8,128)S(1)}, u32[]{:S(2)}, u32[]{:S(2)}) async-start(f32[64,256,32]{1,2,0:T(8,128)} %stack.2), calls=%async_computation.3 | async-start | bytes 4194304 | tf_op jit(solution)/shard_map/all_to_all | solution.py:64
  313.9 1.6 copy.25
  315.4 0.5 broadcast.91
  316.0 0.7 reduce.7
  316.7 0.1 eq.92
  316.8 0.7 reduce.6
  317.6 0.1 eq.96
  317.7 13.1 %copy.40 = f32[16,8,128,128]{3,1,2,0:T(8,128)} copy(f32[16,8,128,128]{3,2,1,0:T(8,128)} %bitcast.55) | data formatting | bytes 16777216
  330.9 9.0 %copy.24 = f32[16384,128]{1,0:T(8,128)} copy(f32[16384,128]{0,1:T(8,128)} %bitcast.57) | data formatting | bytes 16777216 | tf_op jit(solution)/shard_map/dot_general | solution.py:40
  339.9 12.1 %fusion.15 = f32[16,8,128,128]{3,1,2,0:T(8,128)} fusion(f32[128,128,128,1]{2,1,0,3:T(8,128)} %bitcast.56, f32[128,8]{0,1:T(8,128)S(1)} %fusion.25, f32[128,16]{0,1:T(8,128)S(1)} %fusion.24), kind=kOutput, calls=%fused_computation.15 | convolution fusion | flops 3221241856 | bytes 16789504 | tf_op jit(solution)/shard_map/dot_general | solution.py:40
  351.9 16.5 %all-to-all-done.3 = f32[64,256,32]{1,2,0:T(8,128)S(1)} async-done(((f32[64,256,32]{1,2,0:T(8,128)}), f32[64,256,32]{1,2,0:T(8,128)S(1)}, u32[]{:S(2)}, u32[]{:S(2)}) %all-to-all-start.3) | async-done | bytes 2097184 | tf_op jit(solution)/shard_map/all_to_all | solution.py:64
  368.4 17.8 %fusion.8 = f32[256,1024]{0,1:T(8,128)} fusion(f32[256,1024]{0,1:T(8,128)S(1)} %copy.25, f32[256,2048]{0,1:T(8,128)S(1)} %bitcast.58, f32[256,8,8,128]{3,2,1,0:T(8,128)} %bitcast.54), kind=kOutput, calls=%fused_computation.7 | convolution fusion | flops 6442713088 | bytes 12582912 | tf_op jit(solution)/shard_map/dot_general | solution.py:62
  386.2 2.5 copy.26
  (4 shorter events, 0.0 us)
Async XLA Ops:
  6.5 61.3 %all-gather.2.cloned.1.call-start = ((), (), s32[]{:S(2)}) async-start(), calls=%async_computation.4 | async-start | bytes 4718592 | tf_op jit(solution)/shard_map/all_gather | solution.py:51
  11.9 29.2 %all-to-all-start = ((s32[64,1,2]{2,1,0:T(1,128)}), s32[64,1,2]{2,1,0:T(1,128)S(1)}, u32[]{:S(2)}, u32[]{:S(2)}) async-start(s32[64,1,2]{2,1,0:T(1,128)} %copy.20), calls=%async_computation | async-start | bytes 65536 | tf_op jit(solution)/shard_map/all_to_all | solution.py:55
  41.1 43.6 %all-to-all-start.1 = ((s32[64,1,2]{2,1,0:T(1,128)}), s32[64,1,2]{2,1,0:T(1,128)S(1)}, u32[]{:S(2)}, u32[]{:S(2)}) async-start(s32[64,1,2]{2,1,0:T(1,128)} %copy.21), calls=%async_computation.1 | async-start | bytes 65536 | tf_op jit(solution)/shard_map/all_to_all | solution.py:56
  84.7 205.2 %copy-start = (f32[256,32]{0,1:T(8,128)S(1)}, f32[256,32]{0,1:T(8,128)}, u32[]{:S(2)}) copy-start(f32[256,32]{0,1:T(8,128)} %param.7) | copy-start | bytes 98308
  291.5 76.9 %all-to-all-start.3 = ((f32[64,256,32]{1,2,0:T(8,128)}), f32[64,256,32]{1,2,0:T(8,128)S(1)}, u32[]{:S(2)}, u32[]{:S(2)}) async-start(f32[64,256,32]{1,2,0:T(8,128)} %stack.2), calls=%async_computation.3 | async-start | bytes 4194304 | tf_op jit(solution)/shard_map/all_to_all | solution.py:64
Sparse Core Ops, SparseCore 0:
  9.4 58.3 all-gather.1
